TPU v7x, 32 devices: a whole 2x2x4 slice. The times are simulated.
32 devices in a mesh: seq: 4 (over z), exp: 8 (over y, x, core).
Axes of the slice: x: 2, y: 2, z: 4, core: 2. Of those that a mesh axis runs over, the one named last changes fastest.
Arguments:
- queries: bfloat16 [8, 256, 4096], P('exp', 'seq'), may hold values from -30 to 30
- key_heads: bfloat16 [8, 256, 512], P('exp', 'seq'), may hold values from -12 to 12
- value_heads: bfloat16 [8, 256, 512], P('exp', 'seq'), may hold values from -6 to 6
- residual: bfloat16 [8, 256, 4096], P('exp', 'seq'), may hold values from -16 to 16
- lengths: int32 [8, 6], P('exp'), may hold values from 1 to 128, 256 in all within a row
- routes: int32 [8, 256, 4], P('exp', 'seq'), may hold values from 0 to 7, all different within a row; in each aligned block of 64 rows (0 to 63, 64 to 127, ..., all dimensions but the last counted through in order) at most 40 rows name the same one
- gate_weights: bfloat16 [8, 256, 8], P('exp', 'seq'), may hold values from 0.049804688 to 0.29882812
- out_weight: bfloat16 [4096, 4096], P('seq', 'exp'), may hold values from -0.09375 to 0.09375
- norm_gain: float32 [4096], replicated, may hold values from 0.5 to 1.5
- w_gate: bfloat16 [8, 4, 4096, 768], P('exp', 'seq'), may hold values from -0.09375 to 0.09375
- w_up: bfloat16 [8, 4, 4096, 768], P('exp', 'seq'), may hold values from -0.09375 to 0.09375
- w_down: bfloat16 [8, 4, 768, 4096], P('exp', 'seq'), may hold values from -0.15625 to 0.15625
Outputs:
- result: bfloat16 [8, 256, 4096], P('exp', 'seq')
Inputs may be any that keep to these rules, and one draw needn't show every extreme that they name: `lengths`: each row sums to 256, and its largest entry is 128. `routes`: the 4 entries of a token differ; among the rows of one device no column is named more than 40 times, a bound that some block reaches.
All inputs are finite; a program needn't handle non-finite values.
Results may differ from a plain program's by a relative error of at most 0.008.
Values may be sent and summed in bfloat16 or wider, within the bound.
A program may use at most 128 MiB of HBM per device.

v0:
```python
import functools
import math

import jax
import jax.numpy as jnp
from jax import lax
from jax.experimental import pallas as pl
from jax.experimental.pallas import tpu as pltpu
from jax.sharding import PartitionSpec as P

HEAD_DIM = 128
EXP_COL = 2


epsilon = 1e-06


def episode_ids(length_row, position_count):
    bounds = jnp.cumsum(length_row)
    position = jnp.arange(position_count, dtype=jnp.int32)
    return jnp.sum((position[:, None] >= bounds[None, :]).astype(jnp.int32), axis=1)


def attend(query_rows, key_rows, value_rows, episode):
    row_count = query_rows.shape[0]
    groups = key_rows.shape[1] // HEAD_DIM
    per_group = query_rows.shape[1] // HEAD_DIM // groups
    q_heads = query_rows.reshape(row_count, groups, per_group, HEAD_DIM)
    k_heads = key_rows.reshape(row_count, groups, HEAD_DIM)
    v_heads = value_rows.reshape(row_count, groups, HEAD_DIM)
    scores = jnp.einsum(
        "tgpd,ugd->gptu", q_heads, k_heads, preferred_element_type=jnp.float32
    ) / math.sqrt(HEAD_DIM)
    position = jnp.arange(row_count, dtype=jnp.int32)
    allowed = (episode[:, None] == episode[None, :]) & (position[None, :] <= position[:, None])
    scores = jnp.where(allowed, scores, -jnp.inf)
    row_maximum = jnp.max(scores, axis=-1, keepdims=True)
    weights = jnp.exp(scores - row_maximum)
    probability = (weights / jnp.sum(weights, axis=-1, keepdims=True)).astype(jnp.bfloat16)
    mixed = jnp.einsum("gptu,ugd->tgpd", probability, v_heads, preferred_element_type=jnp.float32)
    return mixed.astype(jnp.bfloat16).reshape(row_count, groups * per_group * HEAD_DIM)


def local_routed(
    queries,
    key_heads,
    value_heads,
    residual,
    lengths,
    routes,
    gate_weights,
    out_weight,
    norm_gain,
    w_gate,
    w_up,
    w_down,
):
    seq_count = lax.axis_size("seq")
    columns = lax.axis_size("exp")
    token_count = residual.shape[1]
    model_width = residual.shape[2]
    whole_q, whole_k, whole_v = (
        lax.all_to_all(queries[0], "seq", split_axis=1, concat_axis=0, tiled=True),
        lax.all_to_all(key_heads[0], "seq", split_axis=1, concat_axis=0, tiled=True),
        lax.all_to_all(value_heads[0], "seq", split_axis=1, concat_axis=0, tiled=True),
    )
    episode = episode_ids(lengths[0], whole_q.shape[0])
    mixed = attend(whole_q, whole_k, whole_v, episode)
    head_partial = jnp.dot(
        mixed,
        lax.all_gather(out_weight, "exp", axis=1, tiled=True),
        preferred_element_type=jnp.float32,
    )
    projected = lax.psum_scatter(
        head_partial.astype(jnp.bfloat16), "seq", scatter_dimension=0, tiled=True
    ).astype(jnp.float32)
    hidden = residual[0].astype(jnp.float32) + projected
    inverse = lax.rsqrt(jnp.mean(hidden * hidden, axis=1, keepdims=True) + epsilon)
    normalized_rows = (hidden * inverse * norm_gain[None, :]).astype(jnp.bfloat16)
    routed = routes[0]
    node_count = routed.shape[1]
    capacity = max(2, 5 * token_count * node_count // (4 * columns))
    on_node = routed[:, :, None] == jnp.arange(columns, dtype=jnp.int32)[None, None, :]
    member = jnp.sum(on_node.astype(jnp.int32), axis=1)
    before = jnp.cumsum(member, axis=0) - member
    slot_lookup_index = (
        before[:, :, None] == jnp.arange(capacity, dtype=jnp.int32)[None, None, :]
    ) & (member[:, :, None] > 0)
    slot_flag_mask = slot_lookup_index.astype(jnp.bfloat16)
    outbound = jnp.einsum(
        "roj,rm->ojm", slot_flag_mask, normalized_rows, preferred_element_type=jnp.float32
    ).astype(jnp.bfloat16)
    gate_pair = gate_weights[0].reshape(token_count, node_count, EXP_COL).astype(jnp.float32)
    node_route_gate = jnp.einsum(
        "tnc,tne->tce", on_node.astype(jnp.float32), gate_pair, precision=lax.Precision.HIGHEST
    )
    slot_gate = jnp.einsum(
        "qnr,qny->nry",
        slot_lookup_index.astype(jnp.float32),
        node_route_gate,
        precision=lax.Precision.HIGHEST,
    ).astype(jnp.bfloat16)
    rows_in, gate_in = (
        lax.all_to_all(outbound, "exp", split_axis=0, concat_axis=0, tiled=True),
        lax.all_to_all(slot_gate, "exp", split_axis=0, concat_axis=0, tiled=True),
    )
    rows_all, gate_all = (
        lax.all_gather(rows_in, "seq", axis=0, tiled=True),
        lax.all_gather(gate_in, "seq", axis=0, tiled=True),
    )
    halves = seq_count // EXP_COL
    expert_pick = lax.axis_index("seq") // halves
    flat_rows = rows_all.reshape(-1, model_width)
    flat_gate = lax.dynamic_index_in_dim(
        gate_all.reshape(-1, EXP_COL), expert_pick, axis=1, keepdims=False
    )
    gate_block = w_gate[0, 0]
    up_block = w_up[0, 0]
    down_block = w_down[0, 0]
    gate_proj = jnp.dot(flat_rows, gate_block, preferred_element_type=jnp.float32)
    up_proj = jnp.dot(flat_rows, up_block, preferred_element_type=jnp.float32)
    activated = (jax.nn.silu(gate_proj) * up_proj).astype(jnp.bfloat16)
    partial_value = jnp.dot(activated, down_block, preferred_element_type=jnp.float32).astype(
        jnp.bfloat16
    )
    partial_value = lax.optimization_barrier(partial_value)
    node_sum = lax.psum_scatter(
        (partial_value.astype(jnp.float32) * flat_gate.astype(jnp.float32)[:, None]).astype(
            jnp.bfloat16
        ),
        "seq",
        scatter_dimension=0,
        tiled=True,
    )
    gathered_output = lax.all_to_all(
        node_sum.reshape(columns, capacity, model_width),
        "exp",
        split_axis=0,
        concat_axis=0,
        tiled=True,
    )
    mixture_expert_total = jnp.einsum(
        "gyr,yre->ge", slot_flag_mask, gathered_output, preferred_element_type=jnp.float32
    )
    return (hidden + mixture_expert_total).astype(jnp.bfloat16)[None]

ROWS = 16
CHUNKS = 4
MESH = pl.DeviceIdType.MESH


SCHEDULE = (
    (
        1000, 1010, 1100, 0, 100, 102, 1020, 101, 200, 103, 1120, 1110, 201, 10, 202, 110, 20,
        301, 300, 203, 120, 122, 111, 1030, 302, 303, 400
    ),
    (),
    (113, 210, 112, 123, 1130),
    (121,),
    (211, 30),
    (212, 213),
    (220, 222),
    (900, 132, 311, 310, 130),
    (221, 312, 131, 313),
    (),
    (),
    (500, 410, 133),
    (),
    (223, 502, 321, 322, 320),
    (503,),
    (323, 232, 910),
    (231, 513),
    (233,),
    (512, 603, 420, 511),
    (230,),
    (501,),
    (),
    (),
    (920,),
    (600, 613, 330, 522, 703, 332, 331, 602, 612, 333, 601),
    (521,),
    (713,),
    (430, 611, 510),
    (),
    (523, 712, 621),
    (622, 702),
    (930, 623),
    (
        701, 532, 711, 533, 723, 531, 722, 633, 721, 520, 632, 610, 631, 530, 733, 620, 732, 731,
        810, 630, 820, 800, 830
    ),
)


class Place:
    def __init__(self):
        self.z, self.e = lax.axis_index("seq"), lax.axis_index("exp")
        self.core = lax.rem(self.e, 2)
        x, y = lax.rem(lax.div(self.e, 2), 2), lax.div(self.e, 4)
        self.x, self.y = x, y
        half = lax.div(self.z, 2)
        self.turn = half
        self.mid = self.z + half * (3 - 2 * self.z)
        self.to_x = (self.z, self.e + 2 - 4 * x)
        self.to_y = (self.z, self.e + 4 - 8 * y)
        self.to_core = (self.z, self.e + 1 - 2 * self.core)
        self.order = [self.line(o) for o in (self.mid, 1 - self.mid, 2, 3)]
        self.peers = [(place, self.e) for place in self.order[1:]]
        self.own, self.by_x = y * 2 + x, y * 2 + 1 - x
        self.by_y, self.across = (1 - y) * 2 + x, (1 - y) * 2 + 1 - x

    def line(self, place):
        return place + self.turn * (3 - 2 * place)


def block_kernel(
    chunks,
    size,
    query_ref,
    key_ref,
    value_ref,
    residual_ref,
    length_ref,
    route_ref,
    weight_ref,
    project_ref,
    gain_ref,
    gate_hbm,
    up_hbm,
    down_hbm,
    out_ref,
    queries,
    keys,
    values,
    mixed,
    part,
    from_heads,
    from_near,
    hidden,
    held,
    from_core,
    from_plane,
    from_line,
    w_gate,
    w_up,
    w_down,
    activated,
    load_sem,
    head_send,
    head_recv,
    project_send,
    project_recv,
    part_send,
    part_recv,
    near_recv,
    row_send,
    row_recv,
    core_send,
    core_recv,
    plane_send,
    plane_recv,
    line_send,
    line_recv,
):
    here = Place()
    core = here.core
    width = hidden.shape[1]
    lane_count = lax.axis_size("exp") * EXP_COL
    tokens_here = chunks * size
    units = w_gate.shape[1]
    side = 16 * size

    barrier = pltpu.get_barrier_semaphore()
    for device in (here.to_x, here.to_y, here.to_core, *here.peers):
        pl.semaphore_signal(barrier, inc=1, device_id=device, device_id_type=MESH)

    loads = [
        pltpu.make_async_copy(source, target, load_sem.at[n])
        for n, (source, target) in enumerate(((down_hbm, w_down), (gate_hbm, w_gate), (up_hbm, w_up)))
    ]

    def remote(source, target, sent, got, device):
        return pltpu.make_async_remote_copy(
            src_ref=source,
            dst_ref=target,
            send_sem=sent,
            recv_sem=got,
            device_id=device,
            device_id_type=MESH,
        )

    def slot(which, i, quarter):
        return which * 16 + here.order[i] * 4 + quarter

    def columns_of(k):
        return pl.ds(0, held.shape[2] if k == 0 else width)

    heads = ((key_ref, keys), (value_ref, values), (query_ref, queries))

    def head_block(target, place):
        return target.at[pl.ds(pl.multiple_of(place * tokens_here, tokens_here), tokens_here)]

    def head_columns(source, target, place):
        span = target.shape[1]
        return source.at[:, pl.ds(pl.multiple_of(place * span, span), span)]

    def head_copy(n, i, source_place):
        source, target = heads[n]
        return remote(
            head_columns(source, target, here.order[i]),
            head_block(target, source_place),
            head_send.at[n, i - 1],
            head_recv.at[n, source_place],
            here.peers[i - 1],
        )

    head_loads = [
        pltpu.make_async_copy(
            head_columns(source, target, here.z), head_block(target, here.z), load_sem.at[3 + n]
        )
        for n, (source, target) in enumerate(heads)
    ]

    depth, span = project_ref.shape
    pieces = 4
    piece = depth // pieces

    def project_place(other, x, core, p):
        buffer = w_up if other else w_gate
        start = ((x * 2 + core) * pieces + p) * piece
        return buffer.at[pl.ds(pl.multiple_of(start, piece), piece), pl.ds(0, span)]

    def project_copy(source, other, x, core, p, n, device):
        return remote(
            source,
            project_place(other, x, core, p),
            project_send.at[n],
            project_recv.at[((other * 2 + x) * 2 + core) * pieces + p],
            device,
        )

    def own_piece(p):
        return project_ref.at[pl.ds(p * piece, piece)]

    own_projects = [
        pltpu.make_async_copy(
            own_piece(p), project_place(0, here.x, core, p), load_sem.at[6 + p]
        )
        for p in range(pieces)
    ]

    def got_piece(other, x, core, p):
        place = project_place(other, x, core, p)
        project_copy(place, other, x, core, p, 0, here.to_x).wait_recv()
        return place

    def project_x(p):
        place = got_piece(0, 1 - here.x, core, p)
        if p % 2 == 0:
            project_copy(place, 1, 1 - here.x, core, p, 12 + p // 2, here.to_y).start()
        project_copy(place, 0, 1 - here.x, core, p, 16 + p, here.to_core).start()

    def project_y(p):
        place = got_piece(1, here.x, core, p)
        if p % 2 == 1:
            project_copy(place, 1, here.x, core, p, 14 + p // 2, here.to_x).start()
        project_copy(place, 1, here.x, core, p, 20 + p, here.to_core).start()

    def project_across(p):
        place = got_piece(1, 1 - here.x, core, p)
        project_copy(place, 1, 1 - here.x, core, p, 24 + p, here.to_core).start()

    groups = (
        (0, here.x, here.own),
        (0, 1 - here.x, here.by_x),
        (1, here.x, here.by_y),
        (1, 1 - here.x, here.across),
    )

    def project(g):
        other, x, quarter = groups[g]
        for p in range(pieces):
            got_piece(other, x, 1 - core, p)
        buffer = w_up if other else w_gate

        @pl.loop(0, 4)
        def _(n):
            which, half = lax.div(n, 2), lax.rem(n, 2)
            rows = pl.ds(pl.multiple_of((x * 2 + which) * depth, depth), depth)
            weight = buffer[rows, pl.ds(pl.multiple_of(half * (span // 2), span // 2), span // 2)]
            total = jnp.dot(mixed[...], weight, preferred_element_type=jnp.float32)
            start = pl.multiple_of(quarter * 2 * span + n * (span // 2), span // 2)
            part[:, pl.ds(start, span // 2)] = total.astype(jnp.bfloat16)

    def part_copy(g, i, chunk, source_place, near):
        quarter = groups[g][2]
        columns = pl.ds(pl.multiple_of(quarter * 2 * span, 2 * span), 2 * span)
        count = tokens_here if chunk is None else size
        start = 0 if chunk is None else chunk * size
        n = 0 if chunk is None else 1 + (g - 1) * chunks + chunk
        rows = pl.ds(pl.multiple_of(here.order[i] * tokens_here + start, size), count)
        if near:
            target, got = from_near.at[pl.ds(start, count), columns], near_recv.at[n]
        else:
            target = from_heads.at[source_place, pl.ds(start, count), columns]
            got = part_recv.at[source_place, n]
        device = here.peers[0] if near else here.peers[i - 1]
        return remote(part.at[rows, columns], target, part_send.at[i - 1, n], got, device)

    def send_part(g, chunk=None):
        @pl.when(here.mid == 0)
        def _():
            part_copy(g, 3, chunk, here.z, True).start()

        for i in (2, 1):
            part_copy(g, i, chunk, here.z, False).start()

    def pass_part(g, chunk=None):
        quarter = groups[g][2]
        columns = pl.ds(pl.multiple_of(quarter * 2 * span, 2 * span), 2 * span)
        count = tokens_here if chunk is None else size
        start = 0 if chunk is None else chunk * size
        rows = pl.ds(pl.multiple_of(here.order[3] * tokens_here + start, size), count)

        @pl.when(here.mid == 1)
        def _():
            part_copy(g, 3, chunk, here.z, True).wait_recv()
            total = part[rows, columns].astype(jnp.float32)
            total = total + from_near[pl.ds(start, count), columns].astype(jnp.float32)
            part[rows, columns] = total.astype(jnp.bfloat16)
            part_copy(g, 3, chunk, here.z, False).start()

    def last_groups(k):
        return (1, 2, 3) if k + 1 == chunks else (3,)

    def send_last(k):
        for g in last_groups(k):
            send_part(g, k)

    def pass_last(k):
        for g in last_groups(k):
            pass_part(g, k)

    def attend():
        count = queries.shape[0]
        rows = lax.broadcasted_iota(jnp.int32, (count, count), 0)
        columns = lax.broadcasted_iota(jnp.int32, (count, count), 1)
        row_episode, column_episode = jnp.zeros_like(rows), jnp.zeros_like(rows)
        bound = 0
        for n in range(length_ref.shape[1]):
            bound = bound + length_ref[0, n]
            row_episode += (rows >= bound).astype(jnp.int32)
            column_episode += (columns >= bound).astype(jnp.int32)
        allowed = (row_episode == column_episode) & (columns <= rows)
        kept = jnp.where(allowed, 0.0, -jnp.inf)

        @pl.loop(0, queries.shape[1] // HEAD_DIM)
        def _(head):
            lanes = pl.ds(pl.multiple_of(head * HEAD_DIM, HEAD_DIM), HEAD_DIM)
            scores = lax.dot_general(
                queries[:, lanes],
                keys[...],
                (((1,), (1,)), ((), ())),
                preferred_element_type=jnp.float32,
            )
            scores = scores * (1.0 / math.sqrt(HEAD_DIM)) + kept
            weights = jnp.exp(scores - jnp.max(scores, axis=1, keepdims=True))
            share = (weights / jnp.sum(weights, axis=1, keepdims=True)).astype(jnp.bfloat16)
            value = jnp.dot(share, values[...], preferred_element_type=jnp.float32)
            mixed[:, lanes] = value.astype(jnp.bfloat16)

    def spread_gates():
        lanes = lax.broadcasted_iota(jnp.int32, (size, 128), 1)
        total = jnp.zeros((size, 128), jnp.float32)
        for k in range(chunks):
            routed = route_ref[pl.ds(k * size, size), :]
            gates = weight_ref[pl.ds(k * size, size), :].astype(jnp.float32)
            for n in range(routed.shape[1]):
                for e in range(EXP_COL):
                    lane = k * lane_count + routed[:, n : n + 1] * EXP_COL + e
                    gate = gates[:, EXP_COL * n + e : EXP_COL * n + e + 1]
                    total += jnp.where(lanes == lane, gate, 0.0)
        return total.astype(jnp.bfloat16)

    def normalize(k):
        tokens = pl.ds(k * size, size)

        def got(place):
            if k == 0:
                part_copy(0, 1, None, place, False).wait_recv()
            for g in (1, 2, 3):
                part_copy(g, 1, k, place, False).wait_recv()
            return from_heads[place, tokens, :].astype(jnp.float32)

        mine = pl.ds(pl.multiple_of(here.z * tokens_here + k * size, size), size)
        total = residual_ref[tokens, :].astype(jnp.float32) + part[mine, :].astype(jnp.float32)
        hidden[tokens, :] = total + got(here.order[1]) + got(here.order[2])

        @pl.when(here.mid == 1)
        def _():
            hidden[tokens, :] = hidden[tokens, :] + got(here.order[3])

        total = hidden[tokens, :]
        inverse = lax.rsqrt(jnp.mean(total * total, axis=1, keepdims=True) + epsilon)
        rows = pl.ds(pl.multiple_of(slot(core, 0, here.own) * size, size), size)
        held[k, rows, pl.ds(0, width)] = (total * inverse * gain_ref[...]).astype(jnp.bfloat16)

    for copy in [loads[0], *head_loads, *own_projects]:
        copy.start()
    pl.semaphore_wait(barrier, 6)
    for n in range(3):
        for i in (1, 2, 3):
            head_copy(n, i, here.z).start()
    for p in range(pieces):
        project_copy(own_piece(p), 0, here.x, core, p, p, here.to_x).start()
        project_copy(own_piece(p), 1, here.x, core, p, 4 + p, here.to_y).start()
        project_copy(own_piece(p), 0, here.x, core, p, 8 + p, here.to_core).start()
    for p in range(2):
        project_x(p)
        project_y(p)
    for n in range(3):
        head_loads[n].wait()
        for i in (1, 2, 3):
            head_copy(n, i, here.order[i]).wait_recv()
    attend()
    for copy in own_projects:
        copy.wait()
    project(0)
    send_part(0)
    for p in range(2, pieces):
        project_x(p)
        project_y(p)
    project(1)
    project(2)
    for chunk in range(chunks - 1):
        send_part(1, chunk)
        send_part(2, chunk)
    own_rows = pl.ds(pl.multiple_of(slot(core, 0, here.own) * size, size), size)
    held[0, own_rows, pl.ds(width, 128)] = spread_gates()
    pass_part(0)
    for p in range(2):
        project_across(p)
    for chunk in range(chunks - 1):
        pass_part(1, chunk)
        pass_part(2, chunk)
    for p in range(2, pieces):
        project_across(p)
    project(3)
    for n in range(28):
        project_copy(own_piece(0), 0, here.x, core, 0, n, here.to_x).wait_send()
    for copy in loads[1:]:
        copy.start()

    def row_copy(k, which, n, device):
        block = held.at[k, pl.ds(pl.multiple_of(which * size, size), size), columns_of(k)]
        return pltpu.make_async_remote_copy(
            src_ref=block,
            dst_ref=block,
            send_sem=row_send.at[k, n],
            recv_sem=row_recv.at[k, which],
            device_id=device,
            device_id_type=MESH,
        )

    def send_peers(k):
        normalize(k)
        s = slot(core, 0, here.own)
        row_copy(k, s, 0, here.peers[0]).start()
        row_copy(k, s, 1, here.peers[1]).start()

        @pl.when(here.mid == 1)
        def _():
            row_copy(k, s, 2, here.peers[2]).start()

    def along_line(k, i):
        s = slot(core, i, here.own)
        if i > 0:
            row_copy(k, s, 0, here.peers[0]).wait_recv()
        if i == 3:

            @pl.when(here.mid == 1)
            def _():
                row_copy(k, s, 31, here.peers[0]).start()

        row_copy(k, s, 3 + i, here.to_x).start()
        row_copy(k, s, 9 + i, here.to_y).start()
        row_copy(k, s, 15 + i, here.to_core).start()

    def beside(k, i):
        s = slot(core, i, here.by_x)
        row_copy(k, s, 0, here.to_x).wait_recv()
        if i % 2 == 0:
            row_copy(k, s, 13 + i // 2, here.to_y).start()
        row_copy(k, s, 19 + i, here.to_core).start()
        s = slot(core, i, here.by_y)
        row_copy(k, s, 0, here.to_y).wait_recv()
        if i % 2 == 1:
            row_copy(k, s, 7 + i // 2, here.to_x).start()
        row_copy(k, s, 23 + i, here.to_core).start()

    def across(k, i):
        s = slot(core, i, here.across)
        row_copy(k, s, 0, here.to_x).wait_recv()
        row_copy(k, s, 27 + i, here.to_core).start()

    def all_rows(k):
        @pl.loop(0, 16)
        def _(n):
            row_copy(k, (1 - core) * 16 + n, 0, here.to_core).wait_recv()

    def rows_sent(k):
        for n in (0, 1):
            row_copy(k, 0, n, here.to_core).wait_send()

        @pl.when(here.mid == 1)
        def _():
            for n in (2, 31):
                row_copy(k, 0, n, here.to_core).wait_send()

        @pl.loop(3, 31)
        def _(n):
            row_copy(k, 0, n, here.to_core).wait_send()

    def activate(k, which, tile):
        rows = pl.ds(pl.multiple_of(which * side, side), side)
        columns = pl.ds(tile * 256, 256)
        tokens = held[k, rows, pl.ds(0, width)]
        gates = held[0, rows, pl.ds(width, 128)].astype(jnp.float32)
        lanes = lax.broadcasted_iota(jnp.int32, gates.shape, 1)
        lane = k * lane_count + here.e * EXP_COL + lax.div(here.z, 2)
        scale = jnp.sum(jnp.where(lanes == lane, gates, 0.0), axis=1, keepdims=True)
        gate = jnp.dot(tokens, w_gate[:, columns], preferred_element_type=jnp.float32)
        up = jnp.dot(tokens, w_up[:, columns], preferred_element_type=jnp.float32)
        value = gate / (1.0 + jnp.exp(-gate)) * up * scale
        activated[rows, columns] = value.astype(jnp.bfloat16)

    def lower(k, which):
        rows = pl.ds(pl.multiple_of(which * side, side), side)

        @pl.loop(0, width // 512)
        def _(tile):
            columns = pl.ds(pl.multiple_of(tile * 512, 512), 512)
            part = jnp.dot(activated[rows, :], w_down[:, columns], preferred_element_type=jnp.float32)
            held[k, rows, columns] = part.astype(jnp.bfloat16)

    def core_copy(k, i):
        def group(which):
            return pl.ds(pl.multiple_of((which * 16 + here.order[i] * 4) * size, 4 * size), 4 * size)

        return pltpu.make_async_remote_copy(
            src_ref=held.at[k, group(1 - core), pl.ds(0, width)],
            dst_ref=from_core.at[k, i],
            send_sem=core_send.at[k, i],
            recv_sem=core_recv.at[k, i],
            device_id=here.to_core,
            device_id_type=MESH,
        )

    def mine(k, i, quarter):
        return held.at[
            k, pl.ds(pl.multiple_of(slot(core, i, quarter) * size, size), size), pl.ds(0, width)
        ]

    def both(k, i, quarter):
        other = from_core[k, i, pl.ds(pl.multiple_of(quarter * size, size), size), :]
        return mine(k, i, quarter)[...].astype(jnp.float32) + other.astype(jnp.float32)

    def plane_copy(k, i, kind, quarter, device):
        return pltpu.make_async_remote_copy(
            src_ref=mine(k, i, quarter),
            dst_ref=from_plane.at[k, 4 * kind + i],
            send_sem=plane_send.at[k, 4 * kind + i],
            recv_sem=plane_recv.at[k, 4 * kind + i],
            device_id=device,
            device_id_type=MESH,
        )

    def links(i):
        if i % 2 == 0:
            return here.to_y, here.to_x, here.by_y, here.by_x
        return here.to_x, here.to_y, here.by_x, here.by_y

    def leave(k, i):
        first, _, direct, _ = links(i)
        core_copy(k, i).wait_recv()
        mine(k, i, here.across)[...] = both(k, i, here.across).astype(jnp.bfloat16)
        plane_copy(k, i, 0, here.across, first).start()
        mine(k, i, direct)[...] = both(k, i, direct).astype(jnp.bfloat16)
        plane_copy(k, i, 1, direct, first).start()

    def pass_on(k, i):
        first, second, _, onward = links(i)
        plane_copy(k, i, 0, onward, first).wait_recv()
        total = both(k, i, onward) + from_plane[k, i].astype(jnp.float32)
        mine(k, i, onward)[...] = total.astype(jnp.bfloat16)
        plane_copy(k, i, 2, onward, second).start()

    def line_copy(k, i, source):
        return pltpu.make_async_remote_copy(
            src_ref=mine(k, i, here.own),
            dst_ref=from_line.at[k, source],
            send_sem=line_send.at[k, max(i, 1) - 1],
            recv_sem=line_recv.at[k, source],
            device_id=here.peers[max(i, 1) - 1],
            device_id_type=MESH,
        )

    def line_sum(k, i):
        first, second, _, _ = links(i)
        plane_copy(k, i, 1, here.own, first).wait_recv()
        plane_copy(k, i, 2, here.own, second).wait_recv()
        total = both(k, i, here.own) + from_plane[k, 4 + i].astype(jnp.float32)
        return total + from_plane[k, 8 + i].astype(jnp.float32)

    def send_line(k, i):
        mine(k, i, here.own)[...] = line_sum(k, i).astype(jnp.bfloat16)
        line_copy(k, i, here.z).start()

    def finish(k):
        tokens = pl.ds(pl.multiple_of(k * size, size), size)
        total = hidden[tokens, :] + line_sum(k, 0)
        for source in here.order[1:]:
            line_copy(k, 0, source).wait_recv()
            total = total + from_line[k, source].astype(jnp.float32)
        out_ref[tokens, :] = total.astype(jnp.bfloat16)

    def sums_sent(k):
        for i in range(4):
            core_copy(k, i).wait_send()
            for kind in range(3):
                plane_copy(k, i, kind, here.own, here.to_x).wait_send()
        for i in range(1, 4):
            line_copy(k, i, 0).wait_send()

    def send_core(k):
        for i in (3, 2, 1, 0):
            core_copy(k, i).start()

    moves = (
        lambda k, i: send_peers(k),
        along_line,
        beside,
        across,
        lambda k, i: all_rows(k),
        leave,
        pass_on,
        send_line,
        lambda k, i: finish(k),
        lambda k, i: send_core(k),
        lambda k, i: send_last(k),
        lambda k, i: pass_last(k),
    )

    def run(events):
        for event in events:
            moves[event // 100](event // 10 % 10, event % 10)

    tiles = units // 256
    steps = 2 * tiles + 2
    run(SCHEDULE[0])
    for copy in loads:
        copy.wait()

    @pl.loop(0, chunks)
    def _(k):
        for n in range(steps):
            if n < 2 * tiles:
                activate(k, core if n < tiles else 1 - core, n % tiles)
            elif n == 2 * tiles:
                for chunk in range(chunks):
                    pl.when(k == chunk)(functools.partial(rows_sent, chunk))
                lower(k, 1 - core)
            else:
                lower(k, core)
            for chunk in range(chunks):
                events = SCHEDULE[1 + chunk * steps + n]
                if events:
                    pl.when(k == chunk)(functools.partial(run, events))

    for k in range(chunks):
        sums_sent(k)
    for i in (1, 2, 3):
        for n in range(3):
            head_copy(n, i, here.z).wait_send()
        part_copy(0, i, None, here.z, False).wait_send()
        for g in (1, 2, 3):
            for k in range(chunks):
                part_copy(g, i, k, here.z, False).wait_send()


def local_block(
    queries,
    key_heads,
    value_heads,
    residual,
    lengths,
    routes,
    gate_weights,
    out_weight,
    norm_gain,
    w_gate,
    w_up,
    w_down,
):
    tokens, width = residual.shape[1:]
    line, size = lax.axis_size("seq"), ROWS
    chunks = tokens // size
    units = w_gate.shape[3]
    anywhere = pl.BlockSpec(memory_space=pl.ANY)
    inside = pl.BlockSpec(memory_space=pltpu.VMEM)
    scalars = pl.BlockSpec(memory_space=pltpu.SMEM)
    dma = pltpu.SemaphoreType.DMA
    half = jnp.bfloat16
    head_width, key_width = queries.shape[2] // line, key_heads.shape[2] // line
    whole = line * tokens
    result = pl.pallas_call(
        functools.partial(block_kernel, chunks, size),
        out_shape=jax.ShapeDtypeStruct((tokens, width), half),
        in_specs=[
            anywhere,
            anywhere,
            anywhere,
            inside,
            scalars,
            inside,
            inside,
            anywhere,
            inside,
            anywhere,
            anywhere,
            anywhere,
        ],
        out_specs=inside,
        scratch_shapes=[
            pltpu.VMEM((whole, head_width), half),
            pltpu.VMEM((whole, key_width), half),
            pltpu.VMEM((whole, key_width), half),
            pltpu.VMEM((whole, head_width), half),
            pltpu.VMEM((whole, width), half),
            pltpu.VMEM((line, tokens, width), half),
            pltpu.VMEM((tokens, width), half),
            pltpu.VMEM((tokens, width), jnp.float32),
            pltpu.VMEM((chunks, 32 * size, width + 128), half),
            pltpu.VMEM((chunks, 4, 4 * size, width), half),
            pltpu.VMEM((chunks, 12, size, width), half),
            pltpu.VMEM((chunks, 4, size, width), half),
            pltpu.VMEM(w_gate.shape[2:], half),
            pltpu.VMEM(w_up.shape[2:], half),
            pltpu.VMEM(w_down.shape[2:], half),
            pltpu.VMEM((32 * size, units), half),
            dma((10,)),
            dma((3, 3)),
            dma((3, line)),
            dma((28,)),
            dma((32,)),
            dma((3, 1 + 3 * chunks)),
            dma((line, 1 + 3 * chunks)),
            dma((1 + 3 * chunks,)),
            dma((chunks, 32)),
            dma((chunks, 32)),
            dma((chunks, 4)),
            dma((chunks, 4)),
            dma((chunks, 12)),
            dma((chunks, 12)),
            dma((chunks, 3)),
            dma((chunks, 4)),
        ],
        compiler_params=pltpu.CompilerParams(
            collective_id=0, has_side_effects=True, vmem_limit_bytes=67_000_000
        ),
    )(
        queries[0],
        key_heads[0],
        value_heads[0],
        residual[0],
        lengths,
        routes[0],
        gate_weights[0],
        out_weight,
        norm_gain[None, :],
        w_gate[0, 0],
        w_up[0, 0],
        w_down[0, 0],
    )
    return result[None]


def solution(mesh):
    plane = mesh.shape["exp"] == 8 and mesh.shape["seq"] == 4

    def local(*arguments):
        dense = plane and arguments[3].shape[1] == CHUNKS * ROWS
        return (local_block if dense else local_routed)(*arguments)

    return jax.shard_map(
        local,
        mesh=mesh,
        in_specs=(
            P("exp", "seq", None),
            P("exp", "seq", None),
            P("exp", "seq", None),
            P("exp", "seq", None),
            P("exp", None),
            P("exp", "seq", None),
            P("exp", "seq", None),
            P("seq", "exp"),
            P(),
            P("exp", "seq", None, None),
            P("exp", "seq", None, None),
            P("exp", "seq", None, None),
        ),
        out_specs=P("exp", "seq", None),
        check_vma=False,
    )
```

profile of v0, /device:TPU:1, one launch (start us, length us, event | category | flops | bytes accessed | tf_op | source)
XLA Modules:
  0.0 215.9 jit_solution(1224377735343943396)
XLA Ops:
  0.0 1.4 copy.14
  1.4 1.4 copy.13
  2.7 211.3 %shard_map.118 = bf16[64,4096]{1,0:T(8,128)(2,1)} custom-call(bf16[64,4096]{1,0:T(8,128)(2,1)} %bitcast.15, bf16[64,512]{1,0:T(8,128)(2,1)} %bitcast.18, bf16[64,512]{1,0:T(8,128)(2,1)} %bitcast.19, bf16[64,4096]{1,0:T(8,128)(2,1)} %bitcast.16, s32[1,6]{1,0:T(1,128)} %length_ref.1, s32[64,4]{1,0:T(8,128)} %bitcast.17, bf16[64,8]{1,0:T(8,128)(2,1)} %bitcast.20, ...), custom_call_target="tpu_custom_call" | custom-call | tf_op jit(solution)/shard_map/pallas_call | solution.py:816
  214.1 1.9 copy.16
where the time goes:
time: 216 us
  Pallas kernels  211 us (98%)
  local copies, waits for them, and re-layouts  4.61 us (2%)
    pallas_call x1, Pallas kernels, local_block(): pl.pallas_call(functools.partial(block_kernel, chunks, size), out_shape=j...  211 us
    unnamed x3, local copies, waits for them, and re-layouts  4.61 us

commit v1 on v0

--- a/solution.py
+++ b/solution.py
@@ -149,45 +149,48 @@
 MESH = pl.DeviceIdType.MESH
 
 
+SPREAD = {1: 0, 2: 1, 3: 0}
+
+
 SCHEDULE = (
     (
-        1000, 1010, 1100, 0, 100, 102, 1020, 101, 200, 103, 1120, 1110, 201, 10, 202, 110, 20,
-        301, 300, 203, 120, 122, 111, 1030, 302, 303, 400
+        1000, 1020, 1100, 0, 100, 102, 1010, 101, 200, 103, 1110, 201, 1120, 10, 110, 20, 202,
+        300, 203, 112, 210, 302, 111, 303, 120, 301
     ),
     (),
-    (113, 210, 112, 123, 1130),
-    (121,),
-    (211, 30),
-    (212, 213),
-    (220, 222),
-    (900, 132, 311, 310, 130),
-    (221, 312, 131, 313),
+    (),
+    (113, 400),
+    (310,),
+    (211,),
+    (122,),
+    (1030, 900, 220, 121),
+    (212, 222, 123, 502, 213, 503, 311, 500, 501, 312, 313),
+    (1130,),
+    (320,),
+    (30, 410, 221),
+    (130,),
+    (601, 223),
+    (322, 321),
+    (603, 230, 132),
+    (910, 602, 323),
+    (701, 512, 131),
+    (),
+    (133, 420),
+    (330, 511, 612),
     (),
     (),
-    (500, 410, 133),
+    (513, 510, 920, 600, 332, 233),
+    (333, 232, 231, 611, 610, 331, 702, 703),
+    (613,),
+    (521, 430, 520),
     (),
-    (223, 502, 321, 322, 320),
-    (503,),
-    (323, 232, 910),
-    (231, 513),
-    (233,),
-    (512, 603, 420, 511),
-    (230,),
-    (501,),
+    (713, 523, 522, 712),
     (),
     (),
-    (920,),
-    (600, 613, 330, 522, 703, 332, 331, 602, 612, 333, 601),
-    (521,),
-    (713,),
-    (430, 611, 510),
-    (),
-    (523, 712, 621),
-    (622, 702),
-    (930, 623),
+    (930, 622, 623),
     (
-        701, 532, 711, 533, 723, 531, 722, 633, 721, 520, 632, 610, 631, 530, 733, 620, 732, 731,
-        810, 630, 820, 800, 830
+        621, 533, 711, 531, 722, 532, 633, 723, 632, 721, 810, 631, 530, 800, 733, 620, 732, 731,
+        630, 820, 830
     ),
 )
 
@@ -470,17 +473,24 @@
             mixed[:, lanes] = value.astype(jnp.bfloat16)
 
     def spread_gates():
-        lanes = lax.broadcasted_iota(jnp.int32, (size, 128), 1)
-        total = jnp.zeros((size, 128), jnp.float32)
-        for k in range(chunks):
-            routed = route_ref[pl.ds(k * size, size), :]
-            gates = weight_ref[pl.ds(k * size, size), :].astype(jnp.float32)
-            for n in range(routed.shape[1]):
-                for e in range(EXP_COL):
-                    lane = k * lane_count + routed[:, n : n + 1] * EXP_COL + e
-                    gate = gates[:, EXP_COL * n + e : EXP_COL * n + e + 1]
-                    total += jnp.where(lanes == lane, gate, 0.0)
-        return total.astype(jnp.bfloat16)
+        lanes = lax.broadcasted_iota(jnp.int32, (128, tokens_here), 0)
+        tokens = lax.broadcasted_iota(jnp.int32, (128, tokens_here), 1)
+        first = lax.div(tokens, size) * lane_count
+        total = jnp.zeros(lanes.shape, jnp.float32)
+        for n in range(route_ref.shape[0]):
+            routed = route_ref[n : n + 1, :]
+            for e in range(EXP_COL):
+                gate = weight_ref[EXP_COL * n + e : EXP_COL * n + e + 1, :].astype(jnp.float32)
+                total += jnp.where(lanes == first + routed * EXP_COL + e, gate, 0.0)
+        row = lax.broadcasted_iota(jnp.int32, (size, tokens_here), 0)
+        token = lax.broadcasted_iota(jnp.int32, (size, tokens_here), 1)
+        pick = jnp.where(lax.rem(token, size) == row, 1.0, 0.0).astype(jnp.bfloat16)
+        return lax.dot_general(
+            pick,
+            total.astype(jnp.bfloat16),
+            (((1,), (1,)), ((), ())),
+            preferred_element_type=jnp.float32,
+        ).astype(jnp.bfloat16)
 
     def normalize(k):
         tokens = pl.ds(k * size, size)
@@ -589,18 +599,27 @@
     def beside(k, i):
         s = slot(core, i, here.by_x)
         row_copy(k, s, 0, here.to_x).wait_recv()
-        if i % 2 == 0:
+        if i % 2 == 0 and k not in SPREAD or i == 0 and SPREAD.get(k) == 0:
             row_copy(k, s, 13 + i // 2, here.to_y).start()
         row_copy(k, s, 19 + i, here.to_core).start()
         s = slot(core, i, here.by_y)
         row_copy(k, s, 0, here.to_y).wait_recv()
-        if i % 2 == 1:
+        if i % 2 == 1 and k not in SPREAD or i == 0 and SPREAD.get(k) == 1:
             row_copy(k, s, 7 + i // 2, here.to_x).start()
         row_copy(k, s, 23 + i, here.to_core).start()
 
     def across(k, i):
         s = slot(core, i, here.across)
         row_copy(k, s, 0, here.to_x).wait_recv()
+        if k in SPREAD and i == 0:
+            row_copy(k, s, 32, here.peers[0]).start()
+            row_copy(k, s, 33, here.peers[1]).start()
+        if k in SPREAD and i in (0, 3):
+
+            @pl.when(here.mid == 1)
+            def _():
+                row_copy(k, s, 34 + i // 3, here.peers[2 if i == 0 else 0]).start()
+
         row_copy(k, s, 27 + i, here.to_core).start()
 
     def all_rows(k):
@@ -609,17 +628,19 @@
             row_copy(k, (1 - core) * 16 + n, 0, here.to_core).wait_recv()
 
     def rows_sent(k):
-        for n in (0, 1):
+        always, middle = [0, 1, *range(3, 7), *range(9, 13), *range(15, 31)], [2, 31]
+        if k in SPREAD:
+            always += [32, 33, (13, 7)[SPREAD[k]]]
+            middle += [34, 35]
+        else:
+            always += [7, 8, 13, 14]
+        for n in always:
             row_copy(k, 0, n, here.to_core).wait_send()
 
         @pl.when(here.mid == 1)
         def _():
-            for n in (2, 31):
+            for n in middle:
                 row_copy(k, 0, n, here.to_core).wait_send()
-
-        @pl.loop(3, 31)
-        def _(n):
-            row_copy(k, 0, n, here.to_core).wait_send()
 
     def activate(k, which, tile):
         rows = pl.ds(pl.multiple_of(which * side, side), side)
@@ -856,7 +877,7 @@
             dma((3, 1 + 3 * chunks)),
             dma((line, 1 + 3 * chunks)),
             dma((1 + 3 * chunks,)),
-            dma((chunks, 32)),
+            dma((chunks, 36)),
             dma((chunks, 32)),
             dma((chunks, 4)),
             dma((chunks, 4)),
@@ -874,8 +895,8 @@
         value_heads[0],
         residual[0],
         lengths,
-        routes[0],
-        gate_weights[0],
+        routes[0].T,
+        gate_weights[0].T,
         out_weight,
         norm_gain[None, :],
         w_gate[0, 0],

time: 216 us -> 205 us (0.949)
  Pallas kernels: 211 us -> 203 us
  local copies, waits for them, and re-layouts: 4.61 us -> 1.87 us
    pallas_call x1, Pallas kernels: 211 us -> 203 us  [local_block(): pl.pallas_call(functools.partial(block_kernel, chunks, size), out_shape=j...]
    unnamed x3 -> x1, local copies, waits for them, and re-layouts: 4.61 us -> 1.87 us
where the time goes in v1:
time: 205 us; the launch traced here: 204 us
  Pallas kernels  203 us (99%)
    pallas_call x1, Pallas kernels, local_block(): pl.pallas_call(functools.partial(block_kernel, chunks, size), out_shape=j...  203 us

profile of v1, /device:TPU:1, one launch (start us, length us, event | category | flops | bytes accessed | tf_op | source)
XLA Modules:
  0.0 204.5 jit_solution(1750535659251300877)
XLA Ops:
  0.0 202.6 %shard_map.118 = bf16[64,4096]{1,0:T(8,128)(2,1)} custom-call(bf16[64,4096]{1,0:T(8,128)(2,1)} %bitcast.19, bf16[64,512]{1,0:T(8,128)(2,1)} %bitcast.21, bf16[64,512]{1,0:T(8,128)(2,1)} %bitcast.22, bf16[64,4096]{1,0:T(8,128)(2,1)} %bitcast.20, s32[1,6]{1,0:T(1,128)} %length_ref.1, s32[4,64]{1,0:T(4,128)} %bitcast.24, bf16[8,64]{1,0:T(8,128)(2,1)} %bitcast.25, ...), custom_call_target="tpu_custom_call" | custom-call | tf_op jit(solution)/shard_map/pallas_call | solution.py:837
  202.6 1.9 copy.14

commit v2 on v1

--- a/solution.py
+++ b/solution.py
@@ -149,48 +149,51 @@
 MESH = pl.DeviceIdType.MESH
 
 
+GATHER = {2: 0}
+
+
 SPREAD = {1: 0, 2: 1, 3: 0}
 
 
 SCHEDULE = (
     (
-        1000, 1020, 1100, 0, 100, 102, 1010, 101, 200, 103, 1110, 201, 1120, 10, 110, 20, 202,
-        300, 203, 112, 210, 302, 111, 303, 120, 301
+        1000, 1100, 1020, 0, 1010, 100, 102, 101, 200, 1120, 1110, 103, 10, 20, 202, 201, 300,
+        203, 110, 301, 302, 120, 303
     ),
     (),
-    (),
-    (113, 400),
-    (310,),
-    (211,),
-    (122,),
-    (1030, 900, 220, 121),
-    (212, 222, 123, 502, 213, 503, 311, 500, 501, 312, 313),
-    (1130,),
-    (320,),
-    (30, 410, 221),
-    (130,),
-    (601, 223),
-    (322, 321),
-    (603, 230, 132),
-    (910, 602, 323),
-    (701, 512, 131),
-    (),
-    (133, 420),
-    (330, 511, 612),
+    (210, 122, 1030),
+    (400, 121, 113, 112, 111, 220, 310),
     (),
     (),
-    (513, 510, 920, 600, 332, 233),
-    (333, 232, 231, 611, 610, 331, 702, 703),
-    (613,),
-    (521, 430, 520),
     (),
-    (713, 523, 522, 712),
+    (900,),
+    (123, 311, 503, 222, 212, 1130, 502, 221, 500, 213, 211, 312, 501, 313),
+    (320, 30, 130),
+    (410,),
     (),
     (),
-    (930, 622, 623),
+    (223,),
+    (),
+    (603,),
+    (602, 230, 321, 322, 323),
+    (132, 420, 910, 133),
+    (330,),
+    (131, 703, 513, 232),
+    (511, 512, 510),
+    (231,),
+    (233,),
+    (702, 333, 920, 613, 601, 332, 331),
+    (610, 523),
+    (522,),
+    (521, 430, 621),
+    (713, 612),
+    (520, 701),
+    (622, 600),
+    (623,),
+    (611, 712, 930, 1220),
     (
-        621, 533, 711, 531, 722, 532, 633, 723, 632, 721, 810, 631, 530, 800, 733, 620, 732, 731,
-        630, 820, 830
+        533, 722, 531, 532, 711, 723, 721, 633, 631, 800, 632, 620, 733, 530, 810, 731, 732, 630,
+        820, 830
     ),
 )
 
@@ -696,23 +699,48 @@
             device_id_type=MESH,
         )
 
-    def links(i):
-        if i % 2 == 0:
+    def links(k, i):
+        if (i % 2 if i or k not in GATHER else GATHER[k]) == 0:
             return here.to_y, here.to_x, here.by_y, here.by_x
         return here.to_x, here.to_y, here.by_x, here.by_y
 
+    def cross_copy(k, i, source, target):
+        place = 1 + lax.rem(source - target + 3, 4)
+        return remote(
+            mine(k, i, here.across),
+            from_plane.at[k, place],
+            plane_send.at[k, i],
+            plane_recv.at[k, place],
+            here.peers[i - 1],
+        )
+
     def leave(k, i):
-        first, _, direct, _ = links(i)
+        first, _, direct, _ = links(k, i)
         core_copy(k, i).wait_recv()
-        mine(k, i, here.across)[...] = both(k, i, here.across).astype(jnp.bfloat16)
-        plane_copy(k, i, 0, here.across, first).start()
+        if k not in GATHER or i > 0:
+            mine(k, i, here.across)[...] = both(k, i, here.across).astype(jnp.bfloat16)
+            if k in GATHER:
+                cross_copy(k, i, here.z, here.order[i]).start()
+            else:
+                plane_copy(k, i, 0, here.across, first).start()
         mine(k, i, direct)[...] = both(k, i, direct).astype(jnp.bfloat16)
         plane_copy(k, i, 1, direct, first).start()
 
+    def gather(k):
+        total = both(k, 0, here.across)
+        for i in (1, 2, 3):
+            cross_copy(k, i, here.order[i], here.z).wait_recv()
+            place = 1 + lax.rem(here.order[i] - here.z + 3, 4)
+            total = total + from_plane[k, place].astype(jnp.float32)
+        mine(k, 0, here.across)[...] = total.astype(jnp.bfloat16)
+        plane_copy(k, 0, 0, here.across, links(k, 0)[0]).start()
+
     def pass_on(k, i):
-        first, second, _, onward = links(i)
-        plane_copy(k, i, 0, onward, first).wait_recv()
-        total = both(k, i, onward) + from_plane[k, i].astype(jnp.float32)
+        first, second, _, onward = links(k, i)
+        total = both(k, i, onward)
+        if k not in GATHER or i == 0:
+            plane_copy(k, i, 0, onward, first).wait_recv()
+            total = total + from_plane[k, i].astype(jnp.float32)
         mine(k, i, onward)[...] = total.astype(jnp.bfloat16)
         plane_copy(k, i, 2, onward, second).start()
 
@@ -727,7 +755,7 @@
         )
 
     def line_sum(k, i):
-        first, second, _, _ = links(i)
+        first, second, _, _ = links(k, i)
         plane_copy(k, i, 1, here.own, first).wait_recv()
         plane_copy(k, i, 2, here.own, second).wait_recv()
         total = both(k, i, here.own) + from_plane[k, 4 + i].astype(jnp.float32)
@@ -770,6 +798,7 @@
         lambda k, i: send_core(k),
         lambda k, i: send_last(k),
         lambda k, i: pass_last(k),
+        lambda k, i: gather(k),
     )
 
     def run(events):

time: 205 us -> 198 us (0.966); the launches traced: 204 us -> 194 us
  Pallas kernels: 203 us -> 192 us
    pallas_call x1, Pallas kernels: 203 us -> 192 us  [local_block(): pl.pallas_call(functools.partial(block_kernel, chunks, size), out_shape=j...]
where the time goes in v2:
time: 198 us; the launch traced here: 194 us
  Pallas kernels  192 us (97%)
    pallas_call x1, Pallas kernels, local_block(): pl.pallas_call(functools.partial(block_kernel, chunks, size), out_shape=j...  192 us

profile of v2, /device:TPU:1, one launch (start us, length us, event | category | flops | bytes accessed | tf_op | source)
XLA Modules:
  0.0 194.3 jit_solution(18332532866310524975)
XLA Ops:
  0.0 192.5 %shard_map.118 = bf16[64,4096]{1,0:T(8,128)(2,1)} custom-call(bf16[64,4096]{1,0:T(8,128)(2,1)} %bitcast.19, bf16[64,512]{1,0:T(8,128)(2,1)} %bitcast.21, bf16[64,512]{1,0:T(8,128)(2,1)} %bitcast.22, bf16[64,4096]{1,0:T(8,128)(2,1)} %bitcast.20, s32[1,6]{1,0:T(1,128)} %length_ref.1, s32[4,64]{1,0:T(4,128)} %bitcast.24, bf16[8,64]{1,0:T(8,128)(2,1)} %bitcast.25, ...), custom_call_target="tpu_custom_call" | custom-call | tf_op jit(solution)/shard_map/pallas_call | solution.py:866
  192.5 1.9 copy.14
